TPU v7x, 32 devices: a whole 2x2x4 slice. The times are simulated.
32 devices in a mesh: grid: 16 (over z, y, x), band: 2 (over core).
Axes of the slice: x: 2, y: 2, z: 4, core: 2. Of those that a mesh axis runs over, the one named last changes fastest.
Arguments:
- orbitals: float32 [16, 16, 32, 32, 128], P('grid', 'band'), may hold values from -24 to 24, as said below
- potential: float32 [16, 32, 32, 128], P('grid'), may hold values from -1 to 1
Outputs:
- rotated: float32 [16, 16, 32, 32, 128], P('grid', 'band')
Inputs may be any that keep to these rules, and one draw needn't show every extreme that they name: `orbitals`: real-valued orbital samples.
All inputs are finite; a program needn't handle non-finite values.
Results may differ from a plain program's by a relative error of at most 0.00013.
Values sent between devices are 32-bit elements; how exact they have to be, the bound alone decides.
A program may use at most 128 MiB of HBM per device.

v0:
```python
import jax
import jax.numpy as jnp
from jax import lax
from jax.sharding import PartitionSpec as P

COEFFS = (-49.0 / 18.0, 1.5, -0.15, 1.0 / 90.0)
CENTER = 5.75
HALF_WIDTH = 4.75


def shifted(value, axis, steps):
    count = lax.axis_size(axis)
    leading, last = (max(0, -steps), min(count, count - steps))
    return lax.ppermute(value, axis, [(source, source + steps) for source in range(leading, last)])


def layout():
    devices_grid = lax.axis_size("grid")
    parts_x = max(2, devices_grid // 32)
    parts_z = devices_grid // (parts_x * parts_x)
    return (parts_x, parts_x, parts_z)


def neighbour(face_block, stride, keep_it):
    moved = shifted(face_block.reshape(face_block.shape[0], -1), "grid", stride)
    return jnp.where(keep_it, moved, 0.0).reshape(face_block.shape)


def apply_hamil(values_in, local_potential):
    parts_x, parts_y, parts_z = layout()
    grid_index = lax.axis_index("grid")
    pos_z = grid_index % parts_z
    pos_y = grid_index // parts_z % parts_y
    reach_max = len(COEFFS) - 1
    padded = jnp.pad(
        values_in, ((0, 0), (reach_max, reach_max), (reach_max, reach_max), (reach_max, reach_max))
    )
    plan = (
        (1, parts_y * parts_z, True, True),
        (2, parts_z, pos_y > 0, pos_y < parts_y - 1),
        (3, 1, pos_z > 0, pos_z < parts_z - 1),
    )
    for dim_index, stride, keep_lower, keep_upper in plan:
        extent = values_in.shape[dim_index]
        lower_face = neighbour(
            lax.slice_in_dim(values_in, extent - reach_max, extent, axis=dim_index),
            stride,
            keep_lower,
        )
        upper_face = neighbour(
            lax.slice_in_dim(values_in, 0, reach_max, axis=dim_index), -stride, keep_upper
        )
        lower_start = [0, reach_max, reach_max, reach_max]
        upper_start = [0, reach_max, reach_max, reach_max]
        lower_start[dim_index] = 0
        upper_start[dim_index] = reach_max + extent
        padded = lax.dynamic_update_slice(padded, lower_face, lower_start)
        padded = lax.dynamic_update_slice(padded, upper_face, upper_start)
    summed = 3.0 * COEFFS[0] * values_in
    for dim_index in range(1, 4):
        extent = values_in.shape[dim_index]
        for reach in range(1, reach_max + 1):
            upper_start = [0, reach_max, reach_max, reach_max]
            lower_start = [0, reach_max, reach_max, reach_max]
            upper_start[dim_index] = reach_max + reach
            lower_start[dim_index] = reach_max - reach
            upper_part = lax.slice(
                padded, upper_start, [upper_start[k] + values_in.shape[k] for k in range(4)]
            )
            lower_part = lax.slice(
                padded, lower_start, [lower_start[k] + values_in.shape[k] for k in range(4)]
            )
            summed = summed + COEFFS[reach] * (upper_part + lower_part)
    return -0.5 * summed + local_potential[None] * values_in


def chebyshev(start_block, local_potential):
    first_term = (apply_hamil(start_block, local_potential) - CENTER * start_block) / HALF_WIDTH
    return (
        2.0 * (apply_hamil(first_term, local_potential) - CENTER * first_term) / HALF_WIDTH
        - start_block
    )


def on_device(orbitals, potential):
    local_block = orbitals[0]
    local_potential = potential[0]
    band_index = lax.axis_index("band")
    local_count = local_block.shape[0]
    own_filtered = chebyshev(local_block, local_potential)
    gathered = lax.all_gather(own_filtered, "band", axis=0, tiled=True)
    total_orbs = gathered.shape[0]
    flat_all = gathered.reshape(total_orbs, -1)
    volume = flat_all.shape[1] * lax.axis_size("grid")
    partial_value = jnp.einsum("ic,jc->ij", flat_all, flat_all, precision=lax.Precision.HIGHEST)
    gram = lax.psum(partial_value, "grid")
    gram = gram / volume
    factor = jnp.linalg.cholesky(gram)
    weights = jax.scipy.linalg.solve_triangular(
        factor, jnp.eye(total_orbs, dtype=jnp.float32), lower=True
    )
    weight_rows = lax.dynamic_slice_in_dim(weights, band_index * local_count, local_count, 0)
    rotated = jnp.dot(
        weight_rows, flat_all, precision=lax.Precision.HIGHEST, preferred_element_type=jnp.float32
    )
    return rotated.reshape(local_block.shape)[None]


def solution(mesh):
    in_specs = (P("grid", "band", None, None, None), P("grid", None, None, None))
    out_specs = P("grid", "band", None, None, None)
    return jax.shard_map(
        on_device, mesh=mesh, in_specs=in_specs, out_specs=out_specs, check_vma=False
    )
```

profile of v0, /device:TPU:0, one launch (start us, length us, event | category | flops | bytes accessed | tf_op | source)
XLA Modules:
  0.0 975.7 jit_solution(6393854721621182004)
XLA Ops:
  6.5 6.0 copy.68
  13.6 5.7 collective-permute-start.2
  20.2 4.5 collective-permute-start
  27.3 4.7 fusion.60
  32.0 8.5 copy.22
  42.3 2.5 copy.23
  44.7 4.0 collective-permute-start.4
  48.9 9.1 pad.7
  58.0 8.5 copy.26
  71.6 6.2 reshape.117
  77.8 7.9 copy.25
  85.7 6.2 reshape.118
  91.9 17.1 %copy.29 = f32[8,32,32,3]{3,0,2,1:T(8,128)} copy(f32[8,32,32,3]{3,2,1,0:T(8,128)} %reshape.118) | data formatting | bytes 196608 | tf_op jit(solution)/shard_map/reshape | solution.py:26
  109.1 17.4 %dynamic_update_slice.36 = f32[8,38,38,134]{3,0,2,1:T(8,128)} dynamic-update-slice(f32[8,38,38,134]{3,0,2,1:T(8,128)} %pad.7, f32[8,3,32,128]{3,0,2,1:T(8,128)} %bitcast.2, s32[]{:T(128)} %constant.106.clone.1, s32[]{:T(128)} %constant.106.clone.1, s32[]{:T(128)} %constant.107.clone.1, s32[]{:T(128)} %constant.107.clone.1) | dynamic-update-slice | bytes 786436 | tf_op jit(solution)/shard_map/dynamic_update_slice | solution.py:57
  126.4 17.7 %dynamic_update_slice.37 = f32[8,38,38,134]{3,0,2,1:T(8,128)} dynamic-update-slice(f32[8,38,38,134]{3,0,2,1:T(8,128)} %dynamic_update_slice.36, f32[8,3,32,128]{3,0,2,1:T(8,128)S(1)} %bitcast.78, s32[]{:T(128)} %constant.106.clone.1, s32[]{:T(128)} %constant.108.clone.1, s32[]{:T(128)} %constant.107.clone.1, s32[]{:T(128)} %constant.107.clone.1) | dynamic-update-slice | bytes 786436 | tf_op jit(solution)/shard_map/dynamic_update_slice | solution.py:58
  144.1 17.8 %dynamic_update_slice.38 = f32[8,38,38,134]{3,0,2,1:T(8,128)} dynamic-update-slice(f32[8,38,38,134]{3,0,2,1:T(8,128)} %dynamic_update_slice.37, f32[8,32,3,128]{3,0,2,1:T(8,128)S(1)} %bitcast.75, s32[]{:T(128)} %constant.106.clone.1, s32[]{:T(128)} %constant.107.clone.1, s32[]{:T(128)} %constant.106.clone.1, s32[]{:T(128)} %constant.107.clone.1) | dynamic-update-slice | bytes 786436 | tf_op jit(solution)/shard_map/dynamic_update_slice | solution.py:57
  163.0 17.9 %dynamic_update_slice.39 = f32[8,38,38,134]{3,0,2,1:T(8,128)} dynamic-update-slice(f32[8,38,38,134]{3,0,2,1:T(8,128)} %dynamic_update_slice.38, f32[8,32,3,128]{3,0,2,1:T(8,128)S(1)} %bitcast.77, s32[]{:T(128)} %constant.106.clone.1, s32[]{:T(128)} %constant.107.clone.1, s32[]{:T(128)} %constant.108.clone.1, s32[]{:T(128)} %constant.107.clone.1) | dynamic-update-slice | bytes 786436 | tf_op jit(solution)/shard_map/dynamic_update_slice | solution.py:58
  180.8 28.3 %dynamic_update_slice.40 = f32[8,38,38,134]{3,0,2,1:T(8,128)} dynamic-update-slice(f32[8,38,38,134]{3,0,2,1:T(8,128)} %dynamic_update_slice.39, f32[8,32,32,3]{3,0,2,1:T(8,128)} %copy.25, s32[]{:T(128)} %constant.106.clone.1, s32[]{:T(128)} %constant.107.clone.1, s32[]{:T(128)} %constant.107.clone.1, s32[]{:T(128)} %constant.106.clone.1) | dynamic-update-slice | bytes 196612 | tf_op jit(solution)/shard_map/dynamic_update_slice | solution.py:57
  209.1 163.7 %dynamic_update_slice.41 = f32[8,38,38,134]{3,0,2,1:T(8,128)} dynamic-update-slice(f32[8,38,38,134]{3,0,2,1:T(8,128)} %dynamic_update_slice.40, f32[8,32,32,3]{3,0,2,1:T(8,128)} %copy.29, s32[]{:T(128)} %constant.106.clone.1, s32[]{:T(128)} %constant.107.clone.1, s32[]{:T(128)} %constant.107.clone.1, s32[]{:T(128)} %constant.115.clone.1) | dynamic-update-slice | bytes 196612 | tf_op jit(solution)/shard_map/dynamic_update_slice | solution.py:58
  372.8 61.8 %broadcast_multiply_fusion = (f32[8,32,32,128]{3,0,2,1:T(8,128)}, f32[8,32,32,128]{3,0,2,1:T(8,128)}) fusion(f32[32,32,128]{2,1,0:T(8,128)S(1)} %bitcast.73, f32[8,38,38,134]{3,0,2,1:T(8,128)} %dynamic_update_slice.41, f32[1,8,32,32,128]{4,3,2,1,0:T(8,128)} %param.2), kind=kLoop, calls=%fused_computation.67 | loop fusion | flops 35651584 | bytes 88604672 | tf_op jit(solution)/shard_map/div | solution.py:78
  434.6 2.1 fusion.59
  436.7 7.9 fusion.57
  444.7 8.5 copy.30
  453.2 2.1 reshape.110
  457.1 6.1 collective-permute-start.10
  463.2 2.1 fusion.58
  465.3 9.1 pad.8
  474.4 4.9 collective-permute-start.6
  480.6 5.4 collective-permute-start.8
  487.3 8.6 copy.34
  500.7 6.2 reshape.119
  506.9 8.0 copy.33
  514.8 6.2 reshape.120
  521.0 8.1 copy.37
  529.2 17.7 %dynamic_update_slice.42 = f32[8,38,38,134]{3,0,2,1:T(8,128)} dynamic-update-slice(f32[8,38,38,134]{3,0,2,1:T(8,128)} %pad.8, f32[8,3,32,128]{3,0,2,1:T(8,128)S(1)} %bitcast.80, s32[]{:T(128)} %constant.106.clone.1, s32[]{:T(128)} %constant.106.clone.1, s32[]{:T(128)} %constant.107.clone.1, s32[]{:T(128)} %constant.107.clone.1) | dynamic-update-slice | bytes 786436 | tf_op jit(solution)/shard_map/dynamic_update_slice | solution.py:57
  546.9 17.7 %dynamic_update_slice.43 = f32[8,38,38,134]{3,0,2,1:T(8,128)} dynamic-update-slice(f32[8,38,38,134]{3,0,2,1:T(8,128)} %dynamic_update_slice.42, f32[8,3,32,128]{3,0,2,1:T(8,128)S(1)} %bitcast.79, s32[]{:T(128)} %constant.106.clone.1, s32[]{:T(128)} %constant.108.clone.1, s32[]{:T(128)} %constant.107.clone.1, s32[]{:T(128)} %constant.107.clone.1) | dynamic-update-slice | bytes 786436 | tf_op jit(solution)/shard_map/dynamic_update_slice | solution.py:58
  564.6 17.8 %dynamic_update_slice.44 = f32[8,38,38,134]{3,0,2,1:T(8,128)} dynamic-update-slice(f32[8,38,38,134]{3,0,2,1:T(8,128)} %dynamic_update_slice.43, f32[8,32,3,128]{3,0,2,1:T(8,128)S(1)} %bitcast.74, s32[]{:T(128)} %constant.106.clone.1, s32[]{:T(128)} %constant.107.clone.1, s32[]{:T(128)} %constant.106.clone.1, s32[]{:T(128)} %constant.107.clone.1) | dynamic-update-slice | bytes 786436 | tf_op jit(solution)/shard_map/dynamic_update_slice | solution.py:57
  583.5 17.9 %dynamic_update_slice.45 = f32[8,38,38,134]{3,0,2,1:T(8,128)} dynamic-update-slice(f32[8,38,38,134]{3,0,2,1:T(8,128)} %dynamic_update_slice.44, f32[8,32,3,128]{3,0,2,1:T(8,128)S(1)} %bitcast.76, s32[]{:T(128)} %constant.106.clone.1, s32[]{:T(128)} %constant.107.clone.1, s32[]{:T(128)} %constant.108.clone.1, s32[]{:T(128)} %constant.107.clone.1) | dynamic-update-slice | bytes 786436 | tf_op jit(solution)/shard_map/dynamic_update_slice | solution.py:58
  601.3 28.3 %dynamic_update_slice.46 = f32[8,38,38,134]{3,0,2,1:T(8,128)} dynamic-update-slice(f32[8,38,38,134]{3,0,2,1:T(8,128)} %dynamic_update_slice.45, f32[8,32,32,3]{3,0,2,1:T(8,128)} %copy.33, s32[]{:T(128)} %constant.106.clone.1, s32[]{:T(128)} %constant.107.clone.1, s32[]{:T(128)} %constant.107.clone.1, s32[]{:T(128)} %constant.106.clone.1) | dynamic-update-slice | bytes 196612 | tf_op jit(solution)/shard_map/dynamic_update_slice | solution.py:57
  629.6 163.7 %dynamic_update_slice.47 = f32[8,38,38,134]{3,0,2,1:T(8,128)} dynamic-update-slice(f32[8,38,38,134]{3,0,2,1:T(8,128)} %dynamic_update_slice.46, f32[8,32,32,3]{3,0,2,1:T(8,128)} %copy.37, s32[]{:T(128)} %constant.106.clone.1, s32[]{:T(128)} %constant.107.clone.1, s32[]{:T(128)} %constant.107.clone.1, s32[]{:T(128)} %constant.115.clone.1) | dynamic-update-slice | bytes 196612 | tf_op jit(solution)/shard_map/dynamic_update_slice | solution.py:58
  793.3 62.5 %fusion.8 = f32[8,32,32,128]{3,0,2,1:T(8,128)} fusion(f32[8,38,38,134]{3,0,2,1:T(8,128)} %dynamic_update_slice.47, f32[8,32,32,128]{3,0,2,1:T(8,128)} %get-tuple-element.6, f32[32,32,128]{2,1,0:T(8,128)S(1)} %broadcast_multiply_fusion.1, f32[1,8,32,32,128]{4,3,2,1,0:T(8,128)} %param.2), kind=kLoop, calls=%fused_computation.10 | loop fusion | flops 36700160 | bytes 88604672 | tf_op jit(solution)/shard_map/sub | solution.py:80
  855.8 24.7 %all-gather.2.cloned.1.call-done = f32[16,32,32,128]{3,0,2,1:T(8,128)} async-done(((f32[8,32,32,128]{3,0,2,1:T(8,128)}), f32[16,32,32,128]{3,0,2,1:T(8,128)}) %all-gather.2.cloned.1.call-update) | async-done | bytes 8388624 | tf_op jit(solution)/shard_map/all_gather | solution.py:91
  880.5 16.6 %convolution_bitcast_fusion = f32[16,16]{0,1:T(8,128)S(1)} fusion(f32[16,32,32,128]{3,0,2,1:T(8,128)} %all-gather.2.cloned.1.call-done), kind=kOutput, calls=%fused_computation.68 | convolution fusion | flops 402653184 | bytes 8389632 | tf_op jit(solution)/shard_map/ic,jc->ij/dot_general | solution.py:95
  897.0 42.7 %psum.7 = f32[16,16]{0,1:T(8,128)S(1)} all-reduce(f32[16,16]{0,1:T(8,128)S(1)} %convolution_bitcast_fusion), channel_id=1, replica_groups=mesh['grid'=16,'band'=2] {'grid'}, use_global_device_ids=true, to_apply=%region_0.1 | all-reduce | flops 256 | bytes 2048 | tf_op jit(solution)/shard_map/psum | solution.py:96
  944.1 6.1 copy.40
  950.2 4.9 copy.67
  956.6 9.0 fusion.46
  965.7 2.8 copy.42
  (51 shorter events, 28.6 us)
Async XLA Ops:
  6.5 873.9 %all-gather.2.cloned.1.call-start = ((), (), s32[]{:S(2)}) async-start(), calls=%async_computation | async-start | bytes 12582912 | tf_op jit(solution)/shard_map/all_gather | solution.py:91
  12.5 19.5 %copy-start = (f32[1,8,32,32,128]{4,1,3,2,0:T(8,128)}, f32[1,8,32,32,128]{4,1,3,2,0:T(8,128)S(1)}, u32[]{:S(2)}) copy-start(f32[1,8,32,32,128]{4,1,3,2,0:T(8,128)S(1)} %copy.68) | copy-start | bytes 12582916
  13.6 95.4 %collective-permute-start.2 = (f32[8,12288]{1,0:T(8,128)}, f32[8,12288]{1,0:T(8,128)}, u32[]{:S(2)}, u32[]{:S(2)}) collective-permute-start(f32[8,12288]{1,0:T(8,128)} %bitcast.5), channel_id=1, source_target_pairs={{0,8},{2,10},{4,12},{6,14},{8,16},{10,18},{12,20},{14,22},{16,24},... | collective-permute-start | bytes 1179656 | tf_op jit(solution)/shard_map/ppermute | solution.py:14
  20.2 88.9 %collective-permute-start = (f32[8,12288]{1,0:T(8,128)}, f32[8,12288]{1,0:T(8,128)}, u32[]{:S(2)}, u32[]{:S(2)}) collective-permute-start(f32[8,12288]{1,0:T(8,128)} %bitcast.1), channel_id=1, source_target_pairs={{0,16},{2,18},{4,20},{6,22},{8,24},{10,26},{12,28},{14,30},{1,17},... | collective-permute-start | bytes 1179656 | tf_op jit(solution)/shard_map/ppermute | solution.py:14
  24.7 101.7 %collective-permute-start.1 = (f32[8,12288]{1,0:T(8,128)}, f32[8,12288]{1,0:T(8,128)S(1)}, u32[]{:S(2)}, u32[]{:S(2)}) collective-permute-start(f32[8,12288]{1,0:T(8,128)} %bitcast.3), channel_id=1, source_target_pairs={{16,0},{18,2},{20,4},{22,6},{24,8},{26,10},{28,12},{30,14},{17,1},... | collective-permute-start | bytes 1179656 | tf_op jit(solution)/shard_map/ppermute | solution.py:14
  26.0 136.0 %collective-permute-start.3 = (f32[8,12288]{1,0:T(8,128)}, f32[8,12288]{1,0:T(8,128)}, u32[]{:S(2)}, u32[]{:S(2)}) collective-permute-start(f32[8,12288]{1,0:T(8,128)} %bitcast.7), channel_id=1, source_target_pairs={{8,0},{10,2},{12,4},{14,6},{16,8},{18,10},{20,12},{22,14},{24,16},... | collective-permute-start | bytes 1179656 | tf_op jit(solution)/shard_map/ppermute | solution.py:14
  40.6 8.2 copy-start.1
  44.7 25.3 %collective-permute-start.4 = (f32[8,3072]{1,0:T(8,128)}, f32[8,3072]{1,0:T(8,128)}, u32[]{:S(2)}, u32[]{:S(2)}) collective-permute-start(f32[8,3072]{1,0:T(8,128)} %copy.23), channel_id=1, source_target_pairs={{0,2},{2,4},{4,6},{6,8},{8,10},{10,12},{12,14},{14,16},{16,18},{18... | collective-permute-start | bytes 294920 | tf_op jit(solution)/shard_map/ppermute | solution.py:14
  70.0 15.7 %collective-permute-start.5 = (f32[8,3072]{1,0:T(8,128)S(1)}, f32[8,3072]{1,0:T(8,128)S(1)}, u32[]{:S(2)}, u32[]{:S(2)}) collective-permute-start(f32[8,3072]{1,0:T(8,128)S(1)} %copy.27), channel_id=1, source_target_pairs={{2,0},{4,2},{6,4},{8,6},{10,8},{12,10},{14,12},{16,14},{18,16},{20... | collective-permute-start | bytes 294920 | tf_op jit(solution)/shard_map/ppermute | solution.py:14
  457.1 42.2 %collective-permute-start.10 = (f32[8,3072]{1,0:T(8,128)S(1)}, f32[8,3072]{1,0:T(8,128)}, u32[]{:S(2)}, u32[]{:S(2)}) collective-permute-start(f32[8,3072]{1,0:T(8,128)S(1)} %copy.31), channel_id=1, source_target_pairs={{0,2},{2,4},{4,6},{6,8},{8,10},{10,12},{12,14},{14,16},{16,18},{18... | collective-permute-start | bytes 294920 | tf_op jit(solution)/shard_map/ppermute | solution.py:14
  474.4 54.8 %collective-permute-start.6 = (f32[8,12288]{1,0:T(8,128)}, f32[8,12288]{1,0:T(8,128)S(1)}, u32[]{:S(2)}, u32[]{:S(2)}) collective-permute-start(f32[8,12288]{1,0:T(8,128)} %bitcast.10), channel_id=1, source_target_pairs={{0,16},{2,18},{4,20},{6,22},{8,24},{10,26},{12,28},{14,30},{1,17},... | collective-permute-start | bytes 1179656 | tf_op jit(solution)/shard_map/ppermute | solution.py:14
  479.3 67.7 %collective-permute-start.7 = (f32[8,12288]{1,0:T(8,128)}, f32[8,12288]{1,0:T(8,128)S(1)}, u32[]{:S(2)}, u32[]{:S(2)}) collective-permute-start(f32[8,12288]{1,0:T(8,128)} %bitcast.12), channel_id=1, source_target_pairs={{16,0},{18,2},{20,4},{22,6},{24,8},{26,10},{28,12},{30,14},{17,1},... | collective-permute-start | bytes 1179656 | tf_op jit(solution)/shard_map/ppermute | solution.py:14
  480.6 48.6 %collective-permute-start.8 = (f32[8,12288]{1,0:T(8,128)}, f32[8,12288]{1,0:T(8,128)}, u32[]{:S(2)}, u32[]{:S(2)}) collective-permute-start(f32[8,12288]{1,0:T(8,128)} %bitcast.14), channel_id=1, source_target_pairs={{0,8},{2,10},{4,12},{6,14},{8,16},{10,18},{12,20},{14,22},{16,24},... | collective-permute-start | bytes 1179656 | tf_op jit(solution)/shard_map/ppermute | solution.py:14
  486.0 96.4 %collective-permute-start.9 = (f32[8,12288]{1,0:T(8,128)}, f32[8,12288]{1,0:T(8,128)}, u32[]{:S(2)}, u32[]{:S(2)}) collective-permute-start(f32[8,12288]{1,0:T(8,128)} %bitcast.16), channel_id=1, source_target_pairs={{8,0},{10,2},{12,4},{14,6},{16,8},{18,10},{20,12},{22,14},{24,16},... | collective-permute-start | bytes 1179656 | tf_op jit(solution)/shard_map/ppermute | solution.py:14
  499.3 15.5 %collective-permute-start.11 = (f32[8,3072]{1,0:T(8,128)S(1)}, f32[8,3072]{1,0:T(8,128)S(1)}, u32[]{:S(2)}, u32[]{:S(2)}) collective-permute-start(f32[8,3072]{1,0:T(8,128)S(1)} %copy.35), channel_id=1, source_target_pairs={{2,0},{4,2},{6,4},{8,6},{10,8},{12,10},{14,12},{16,14},{18,16},{20... | collective-permute-start | bytes 294920 | tf_op jit(solution)/shard_map/ppermute | solution.py:14
Sparse Core Ops, SparseCore 0:
  855.9 24.4 all-gather.1
where the time goes:
time: 986 us; the launch traced here: 976 us
  local copies, waits for them, and re-layouts  699 us (71%)
  other arithmetic  131 us (13%)
  blocking collectives  42.7 us (4%)
  starting transfers between devices  38.6 us (4%)
  matrix products  25.8 us (3%)
  waiting for transfers between devices  24.7 us (3%)
  between operations  14.2 us (1%)
    dynamic_update_slice x6, local copies, waits for them, and re-layouts, apply_hamil(): padded = lax.dynamic_update_slice(padded, upper_face, upper_start)  398 us
    dynamic_update_slice x6, local copies, waits for them, and re-layouts, apply_hamil(): padded = lax.dynamic_update_slice(padded, lower_face, lower_start)  127 us
    reshape x8, local copies, waits for them, and re-layouts, neighbour(): return jnp.where(keep_it, moved, 0.0).reshape(face_block.shape)  65.9 us
    sub x1, other arithmetic, chebyshev(): 2.0 * (apply_hamil(first_term, local_potential) - CENTER * first_term)  62.5 us
    div x1, other arithmetic, chebyshev(): (apply_hamil(start_block, local_potential) - CENTER * start_block) / HALF...  61.8 us
    psum x1, blocking collectives, on_device(): gram = lax.psum(partial_value, 'grid')  42.7 us
    ppermute x12, starting transfers between devices, shifted(): lax.ppermute(value, axis, [(source, source + steps) for source in range(l...  38.6 us
    slice x8, local copies, waits for them, and re-layouts, apply_hamil(): lax.slice_in_dim(values_in, 0, reach_max, axis=dim_index)  36 us
  transfers between devices with their start and end apart: 13, of which 1 were waited for; matrix products, arithmetic and copies ran while one was open for 24% of the time, Pallas kernels for 0%

commit v1 on v0

--- a/solution.py
+++ b/solution.py
@@ -93,7 +93,7 @@
     flat_all = gathered.reshape(total_orbs, -1)
     volume = flat_all.shape[1] * lax.axis_size("grid")
     partial_value = jnp.einsum("ic,jc->ij", flat_all, flat_all, precision=lax.Precision.HIGHEST)
-    gram = lax.psum(partial_value, "grid")
+    gram = jnp.sum(lax.all_gather(partial_value, "grid"), axis=0)
     gram = gram / volume
     factor = jnp.linalg.cholesky(gram)
     weights = jax.scipy.linalg.solve_triangular(

time: 986 us -> 985 us (level)
    psum x1 -> x0, blocking collectives: 42.7 us -> none  [on_device(): gram = lax.psum(partial_value, 'grid')]
    all_gather x0 -> x1, blocking collectives: none -> 41.9 us  [on_device(): gram = jnp.sum(lax.all_gather(partial_value, 'grid'), axis=0)]
where the time goes in v1:
time: 985 us; the launch traced here: 975 us
  local copies, waits for them, and re-layouts  699 us (71%)
  other arithmetic  131 us (13%)
  blocking collectives  41.9 us (4%)
  starting transfers between devices  38.6 us (4%)
  matrix products  25.4 us (3%)
  waiting for transfers between devices  24.7 us (3%)
  between operations  14.1 us (1%)
    dynamic_update_slice x6, local copies, waits for them, and re-layouts, apply_hamil(): padded = lax.dynamic_update_slice(padded, upper_face, upper_start)  398 us
    dynamic_update_slice x6, local copies, waits for them, and re-layouts, apply_hamil(): padded = lax.dynamic_update_slice(padded, lower_face, lower_start)  127 us
    reshape x8, local copies, waits for them, and re-layouts, neighbour(): return jnp.where(keep_it, moved, 0.0).reshape(face_block.shape)  65.9 us
    sub x1, other arithmetic, chebyshev(): 2.0 * (apply_hamil(first_term, local_potential) - CENTER * first_term)  62.5 us
    div x1, other arithmetic, chebyshev(): (apply_hamil(start_block, local_potential) - CENTER * start_block) / HALF...  61.8 us
    all_gather x1, blocking collectives, on_device(): gram = jnp.sum(lax.all_gather(partial_value, 'grid'), axis=0)  41.9 us
    ppermute x12, starting transfers between devices, shifted(): lax.ppermute(value, axis, [(source, source + steps) for source in range(l...  38.6 us
    slice x8, local copies, waits for them, and re-layouts, apply_hamil(): lax.slice_in_dim(values_in, 0, reach_max, axis=dim_index)  36 us
  transfers between devices with their start and end apart: 13, of which 1 were waited for; matrix products, arithmetic and copies ran while one was open for 24% of the time, Pallas kernels for 0%

profile of v1, /device:TPU:0, one launch (start us, length us, event | category | flops | bytes accessed | tf_op | source)
XLA Modules:
  0.0 974.6 jit_solution(3108298042894450911)
XLA Ops:
  6.5 6.0 copy.64
  13.6 5.7 collective-permute-start.2
  20.2 4.5 collective-permute-start
  27.3 4.7 fusion.60
  32.0 8.5 copy.20
  42.3 2.5 copy.21
  44.7 4.0 collective-permute-start.4
  48.9 9.1 pad.7
  58.0 8.5 copy.24
  71.6 6.2 reshape.118
  77.8 7.9 copy.23
  85.7 6.2 reshape.119
  91.9 17.1 %copy.27 = f32[8,32,32,3]{3,0,2,1:T(8,128)} copy(f32[8,32,32,3]{3,2,1,0:T(8,128)} %reshape.119) | data formatting | bytes 196608 | tf_op jit(solution)/shard_map/reshape | solution.py:26
  109.1 17.4 %dynamic_update_slice.36 = f32[8,38,38,134]{3,0,2,1:T(8,128)} dynamic-update-slice(f32[8,38,38,134]{3,0,2,1:T(8,128)} %pad.7, f32[8,3,32,128]{3,0,2,1:T(8,128)} %bitcast.2, s32[]{:T(128)} %constant.107.clone.1, s32[]{:T(128)} %constant.107.clone.1, s32[]{:T(128)} %constant.108.clone.1, s32[]{:T(128)} %constant.108.clone.1) | dynamic-update-slice | bytes 786436 | tf_op jit(solution)/shard_map/dynamic_update_slice | solution.py:57
  126.4 17.7 %dynamic_update_slice.37 = f32[8,38,38,134]{3,0,2,1:T(8,128)} dynamic-update-slice(f32[8,38,38,134]{3,0,2,1:T(8,128)} %dynamic_update_slice.36, f32[8,3,32,128]{3,0,2,1:T(8,128)S(1)} %bitcast.82, s32[]{:T(128)} %constant.107.clone.1, s32[]{:T(128)} %constant.109.clone.1, s32[]{:T(128)} %constant.108.clone.1, s32[]{:T(128)} %constant.108.clone.1) | dynamic-update-slice | bytes 786436 | tf_op jit(solution)/shard_map/dynamic_update_slice | solution.py:58
  144.1 17.8 %dynamic_update_slice.38 = f32[8,38,38,134]{3,0,2,1:T(8,128)} dynamic-update-slice(f32[8,38,38,134]{3,0,2,1:T(8,128)} %dynamic_update_slice.37, f32[8,32,3,128]{3,0,2,1:T(8,128)S(1)} %bitcast.78, s32[]{:T(128)} %constant.107.clone.1, s32[]{:T(128)} %constant.108.clone.1, s32[]{:T(128)} %constant.107.clone.1, s32[]{:T(128)} %constant.108.clone.1) | dynamic-update-slice | bytes 786436 | tf_op jit(solution)/shard_map/dynamic_update_slice | solution.py:57
  163.0 17.9 %dynamic_update_slice.39 = f32[8,38,38,134]{3,0,2,1:T(8,128)} dynamic-update-slice(f32[8,38,38,134]{3,0,2,1:T(8,128)} %dynamic_update_slice.38, f32[8,32,3,128]{3,0,2,1:T(8,128)S(1)} %bitcast.80, s32[]{:T(128)} %constant.107.clone.1, s32[]{:T(128)} %constant.108.clone.1, s32[]{:T(128)} %constant.109.clone.1, s32[]{:T(128)} %constant.108.clone.1) | dynamic-update-slice | bytes 786436 | tf_op jit(solution)/shard_map/dynamic_update_slice | solution.py:58
  180.8 28.3 %dynamic_update_slice.40 = f32[8,38,38,134]{3,0,2,1:T(8,128)} dynamic-update-slice(f32[8,38,38,134]{3,0,2,1:T(8,128)} %dynamic_update_slice.39, f32[8,32,32,3]{3,0,2,1:T(8,128)} %copy.23, s32[]{:T(128)} %constant.107.clone.1, s32[]{:T(128)} %constant.108.clone.1, s32[]{:T(128)} %constant.108.clone.1, s32[]{:T(128)} %constant.107.clone.1) | dynamic-update-slice | bytes 196612 | tf_op jit(solution)/shard_map/dynamic_update_slice | solution.py:57
  209.1 163.7 %dynamic_update_slice.41 = f32[8,38,38,134]{3,0,2,1:T(8,128)} dynamic-update-slice(f32[8,38,38,134]{3,0,2,1:T(8,128)} %dynamic_update_slice.40, f32[8,32,32,3]{3,0,2,1:T(8,128)} %copy.27, s32[]{:T(128)} %constant.107.clone.1, s32[]{:T(128)} %constant.108.clone.1, s32[]{:T(128)} %constant.108.clone.1, s32[]{:T(128)} %constant.116.clone.1) | dynamic-update-slice | bytes 196612 | tf_op jit(solution)/shard_map/dynamic_update_slice | solution.py:58
  372.8 61.8 %broadcast_multiply_fusion = (f32[8,32,32,128]{3,0,2,1:T(8,128)}, f32[8,32,32,128]{3,0,2,1:T(8,128)}) fusion(f32[32,32,128]{2,1,0:T(8,128)S(1)} %bitcast.76, f32[8,38,38,134]{3,0,2,1:T(8,128)} %dynamic_update_slice.41, f32[1,8,32,32,128]{4,3,2,1,0:T(8,128)} %param.2), kind=kLoop, calls=%fused_computation.67 | loop fusion | flops 35651584 | bytes 88604672 | tf_op jit(solution)/shard_map/div | solution.py:78
  434.6 2.1 fusion.59
  436.7 7.9 fusion.57
  444.7 8.5 copy.28
  453.2 2.1 reshape.110
  457.1 6.1 collective-permute-start.10
  463.2 2.1 fusion.58
  465.3 9.1 pad.8
  474.4 4.9 collective-permute-start.6
  480.6 5.4 collective-permute-start.8
  487.3 8.6 copy.32
  500.7 6.2 reshape.120
  506.9 8.0 copy.31
  514.8 6.2 reshape.121
  521.0 8.1 copy.35
  529.2 17.7 %dynamic_update_slice.42 = f32[8,38,38,134]{3,0,2,1:T(8,128)} dynamic-update-slice(f32[8,38,38,134]{3,0,2,1:T(8,128)} %pad.8, f32[8,3,32,128]{3,0,2,1:T(8,128)S(1)} %bitcast.84, s32[]{:T(128)} %constant.107.clone.1, s32[]{:T(128)} %constant.107.clone.1, s32[]{:T(128)} %constant.108.clone.1, s32[]{:T(128)} %constant.108.clone.1) | dynamic-update-slice | bytes 786436 | tf_op jit(solution)/shard_map/dynamic_update_slice | solution.py:57
  546.9 17.7 %dynamic_update_slice.43 = f32[8,38,38,134]{3,0,2,1:T(8,128)} dynamic-update-slice(f32[8,38,38,134]{3,0,2,1:T(8,128)} %dynamic_update_slice.42, f32[8,3,32,128]{3,0,2,1:T(8,128)S(1)} %bitcast.83, s32[]{:T(128)} %constant.107.clone.1, s32[]{:T(128)} %constant.109.clone.1, s32[]{:T(128)} %constant.108.clone.1, s32[]{:T(128)} %constant.108.clone.1) | dynamic-update-slice | bytes 786436 | tf_op jit(solution)/shard_map/dynamic_update_slice | solution.py:58
  564.6 17.8 %dynamic_update_slice.44 = f32[8,38,38,134]{3,0,2,1:T(8,128)} dynamic-update-slice(f32[8,38,38,134]{3,0,2,1:T(8,128)} %dynamic_update_slice.43, f32[8,32,3,128]{3,0,2,1:T(8,128)S(1)} %bitcast.77, s32[]{:T(128)} %constant.107.clone.1, s32[]{:T(128)} %constant.108.clone.1, s32[]{:T(128)} %constant.107.clone.1, s32[]{:T(128)} %constant.108.clone.1) | dynamic-update-slice | bytes 786436 | tf_op jit(solution)/shard_map/dynamic_update_slice | solution.py:57
  583.5 17.9 %dynamic_update_slice.45 = f32[8,38,38,134]{3,0,2,1:T(8,128)} dynamic-update-slice(f32[8,38,38,134]{3,0,2,1:T(8,128)} %dynamic_update_slice.44, f32[8,32,3,128]{3,0,2,1:T(8,128)S(1)} %bitcast.79, s32[]{:T(128)} %constant.107.clone.1, s32[]{:T(128)} %constant.108.clone.1, s32[]{:T(128)} %constant.109.clone.1, s32[]{:T(128)} %constant.108.clone.1) | dynamic-update-slice | bytes 786436 | tf_op jit(solution)/shard_map/dynamic_update_slice | solution.py:58
  601.3 28.3 %dynamic_update_slice.46 = f32[8,38,38,134]{3,0,2,1:T(8,128)} dynamic-update-slice(f32[8,38,38,134]{3,0,2,1:T(8,128)} %dynamic_update_slice.45, f32[8,32,32,3]{3,0,2,1:T(8,128)} %copy.31, s32[]{:T(128)} %constant.107.clone.1, s32[]{:T(128)} %constant.108.clone.1, s32[]{:T(128)} %constant.108.clone.1, s32[]{:T(128)} %constant.107.clone.1) | dynamic-update-slice | bytes 196612 | tf_op jit(solution)/shard_map/dynamic_update_slice | solution.py:57
  629.6 163.7 %dynamic_update_slice.47 = f32[8,38,38,134]{3,0,2,1:T(8,128)} dynamic-update-slice(f32[8,38,38,134]{3,0,2,1:T(8,128)} %dynamic_update_slice.46, f32[8,32,32,3]{3,0,2,1:T(8,128)} %copy.35, s32[]{:T(128)} %constant.107.clone.1, s32[]{:T(128)} %constant.108.clone.1, s32[]{:T(128)} %constant.108.clone.1, s32[]{:T(128)} %constant.116.clone.1) | dynamic-update-slice | bytes 196612 | tf_op jit(solution)/shard_map/dynamic_update_slice | solution.py:58
  793.3 62.5 %fusion.8 = f32[8,32,32,128]{3,0,2,1:T(8,128)} fusion(f32[8,38,38,134]{3,0,2,1:T(8,128)} %dynamic_update_slice.47, f32[8,32,32,128]{3,0,2,1:T(8,128)} %get-tuple-element.6, f32[32,32,128]{2,1,0:T(8,128)S(1)} %broadcast_multiply_fusion.1, f32[1,8,32,32,128]{4,3,2,1,0:T(8,128)} %param.2), kind=kLoop, calls=%fused_computation.10 | loop fusion | flops 36700160 | bytes 88604672 | tf_op jit(solution)/shard_map/sub | solution.py:80
  855.8 24.7 %all-gather.3.cloned.1.call-done = f32[16,32,32,128]{3,0,2,1:T(8,128)} async-done(((f32[8,32,32,128]{3,0,2,1:T(8,128)}), f32[16,32,32,128]{3,0,2,1:T(8,128)}) %all-gather.3.cloned.1.call-update) | async-done | bytes 8388624 | tf_op jit(solution)/shard_map/all_gather | solution.py:91
  880.5 16.2 %convolution_bitcast_fusion = f32[16,16]{1,0:T(8,128)S(1)} fusion(f32[16,32,32,128]{3,0,2,1:T(8,128)} %all-gather.3.cloned.1.call-done), kind=kOutput, calls=%fused_computation.68 | convolution fusion | flops 402653184 | bytes 8389632 | tf_op jit(solution)/shard_map/ic,jc->ij/dot_general | solution.py:95
  896.6 41.9 %all-gather = f32[256,16]{1,0:T(8,128)S(1)} all-gather(f32[16,16]{1,0:T(8,128)S(1)} %convolution_bitcast_fusion), channel_id=2, replica_groups=mesh['grid'=16,'band'=2] {'grid'}, dimensions={0}, use_global_device_ids=true | all-gather | bytes 17408 | tf_op jit(solution)/shard_map/all_gather | solution.py:96
  942.9 6.1 copy.37
  949.0 4.9 copy.63
  955.5 9.0 fusion.46
  964.5 2.8 copy.39
  (51 shorter events, 28.6 us)
Async XLA Ops:
  6.5 873.9 %all-gather.3.cloned.1.call-start = ((), (), s32[]{:S(2)}) async-start(), calls=%async_computation | async-start | bytes 12582912 | tf_op jit(solution)/shard_map/all_gather | solution.py:91
  12.5 19.5 %copy-start = (f32[1,8,32,32,128]{4,1,3,2,0:T(8,128)}, f32[1,8,32,32,128]{4,1,3,2,0:T(8,128)S(1)}, u32[]{:S(2)}) copy-start(f32[1,8,32,32,128]{4,1,3,2,0:T(8,128)S(1)} %copy.64) | copy-start | bytes 12582916
  13.6 95.4 %collective-permute-start.2 = (f32[8,12288]{1,0:T(8,128)}, f32[8,12288]{1,0:T(8,128)}, u32[]{:S(2)}, u32[]{:S(2)}) collective-permute-start(f32[8,12288]{1,0:T(8,128)} %bitcast.5), channel_id=1, source_target_pairs={{0,8},{2,10},{4,12},{6,14},{8,16},{10,18},{12,20},{14,22},{16,24},... | collective-permute-start | bytes 1179656 | tf_op jit(solution)/shard_map/ppermute | solution.py:14
  20.2 88.9 %collective-permute-start = (f32[8,12288]{1,0:T(8,128)}, f32[8,12288]{1,0:T(8,128)}, u32[]{:S(2)}, u32[]{:S(2)}) collective-permute-start(f32[8,12288]{1,0:T(8,128)} %bitcast.1), channel_id=1, source_target_pairs={{0,16},{2,18},{4,20},{6,22},{8,24},{10,26},{12,28},{14,30},{1,17},... | collective-permute-start | bytes 1179656 | tf_op jit(solution)/shard_map/ppermute | solution.py:14
  24.7 101.7 %collective-permute-start.1 = (f32[8,12288]{1,0:T(8,128)}, f32[8,12288]{1,0:T(8,128)S(1)}, u32[]{:S(2)}, u32[]{:S(2)}) collective-permute-start(f32[8,12288]{1,0:T(8,128)} %bitcast.3), channel_id=1, source_target_pairs={{16,0},{18,2},{20,4},{22,6},{24,8},{26,10},{28,12},{30,14},{17,1},... | collective-permute-start | bytes 1179656 | tf_op jit(solution)/shard_map/ppermute | solution.py:14
  26.0 136.0 %collective-permute-start.3 = (f32[8,12288]{1,0:T(8,128)}, f32[8,12288]{1,0:T(8,128)}, u32[]{:S(2)}, u32[]{:S(2)}) collective-permute-start(f32[8,12288]{1,0:T(8,128)} %bitcast.7), channel_id=1, source_target_pairs={{8,0},{10,2},{12,4},{14,6},{16,8},{18,10},{20,12},{22,14},{24,16},... | collective-permute-start | bytes 1179656 | tf_op jit(solution)/shard_map/ppermute | solution.py:14
  40.6 8.2 copy-start.1
  44.7 25.3 %collective-permute-start.4 = (f32[8,3072]{1,0:T(8,128)}, f32[8,3072]{1,0:T(8,128)}, u32[]{:S(2)}, u32[]{:S(2)}) collective-permute-start(f32[8,3072]{1,0:T(8,128)} %copy.21), channel_id=1, source_target_pairs={{0,2},{2,4},{4,6},{6,8},{8,10},{10,12},{12,14},{14,16},{16,18},{18... | collective-permute-start | bytes 294920 | tf_op jit(solution)/shard_map/ppermute | solution.py:14
  70.0 15.7 %collective-permute-start.5 = (f32[8,3072]{1,0:T(8,128)S(1)}, f32[8,3072]{1,0:T(8,128)S(1)}, u32[]{:S(2)}, u32[]{:S(2)}) collective-permute-start(f32[8,3072]{1,0:T(8,128)S(1)} %copy.25), channel_id=1, source_target_pairs={{2,0},{4,2},{6,4},{8,6},{10,8},{12,10},{14,12},{16,14},{18,16},{20... | collective-permute-start | bytes 294920 | tf_op jit(solution)/shard_map/ppermute | solution.py:14
  457.1 42.2 %collective-permute-start.10 = (f32[8,3072]{1,0:T(8,128)S(1)}, f32[8,3072]{1,0:T(8,128)}, u32[]{:S(2)}, u32[]{:S(2)}) collective-permute-start(f32[8,3072]{1,0:T(8,128)S(1)} %copy.29), channel_id=1, source_target_pairs={{0,2},{2,4},{4,6},{6,8},{8,10},{10,12},{12,14},{14,16},{16,18},{18... | collective-permute-start | bytes 294920 | tf_op jit(solution)/shard_map/ppermute | solution.py:14
  474.4 54.8 %collective-permute-start.6 = (f32[8,12288]{1,0:T(8,128)}, f32[8,12288]{1,0:T(8,128)S(1)}, u32[]{:S(2)}, u32[]{:S(2)}) collective-permute-start(f32[8,12288]{1,0:T(8,128)} %bitcast.10), channel_id=1, source_target_pairs={{0,16},{2,18},{4,20},{6,22},{8,24},{10,26},{12,28},{14,30},{1,17},... | collective-permute-start | bytes 1179656 | tf_op jit(solution)/shard_map/ppermute | solution.py:14
  479.3 67.7 %collective-permute-start.7 = (f32[8,12288]{1,0:T(8,128)}, f32[8,12288]{1,0:T(8,128)S(1)}, u32[]{:S(2)}, u32[]{:S(2)}) collective-permute-start(f32[8,12288]{1,0:T(8,128)} %bitcast.12), channel_id=1, source_target_pairs={{16,0},{18,2},{20,4},{22,6},{24,8},{26,10},{28,12},{30,14},{17,1},... | collective-permute-start | bytes 1179656 | tf_op jit(solution)/shard_map/ppermute | solution.py:14
  480.6 48.6 %collective-permute-start.8 = (f32[8,12288]{1,0:T(8,128)}, f32[8,12288]{1,0:T(8,128)}, u32[]{:S(2)}, u32[]{:S(2)}) collective-permute-start(f32[8,12288]{1,0:T(8,128)} %bitcast.14), channel_id=1, source_target_pairs={{0,8},{2,10},{4,12},{6,14},{8,16},{10,18},{12,20},{14,22},{16,24},... | collective-permute-start | bytes 1179656 | tf_op jit(solution)/shard_map/ppermute | solution.py:14
  486.0 96.4 %collective-permute-start.9 = (f32[8,12288]{1,0:T(8,128)}, f32[8,12288]{1,0:T(8,128)}, u32[]{:S(2)}, u32[]{:S(2)}) collective-permute-start(f32[8,12288]{1,0:T(8,128)} %bitcast.16), channel_id=1, source_target_pairs={{8,0},{10,2},{12,4},{14,6},{16,8},{18,10},{20,12},{22,14},{24,16},... | collective-permute-start | bytes 1179656 | tf_op jit(solution)/shard_map/ppermute | solution.py:14
  499.3 15.5 %collective-permute-start.11 = (f32[8,3072]{1,0:T(8,128)S(1)}, f32[8,3072]{1,0:T(8,128)S(1)}, u32[]{:S(2)}, u32[]{:S(2)}) collective-permute-start(f32[8,3072]{1,0:T(8,128)S(1)} %copy.33), channel_id=1, source_target_pairs={{2,0},{4,2},{6,4},{8,6},{10,8},{12,10},{14,12},{16,14},{18,16},{20... | collective-permute-start | bytes 294920 | tf_op jit(solution)/shard_map/ppermute | solution.py:14
Sparse Core Ops, SparseCore 0:
  855.9 24.4 all-gather.2
